TPU v7x, 32 devices: a whole 2x2x4 slice. The times are simulated.
32 devices in a mesh: tgt: 2 (over core), sup: 16 (over z, y, x).
Axes of the slice: x: 2, y: 2, z: 4, core: 2. Of those that a mesh axis runs over, the one named last changes fastest.
Arguments:
- image_pool: bfloat16 [2048, 3072], P(('tgt', 'sup')), may hold values from -1 to 2
- target_index: int32 [64], replicated, may hold values from 0 to 2047, as said below
- labels: int32 [64], P('tgt'), may hold values from 0 to 1023
- support: float32 [64, 3, 1024], P('sup'), may hold values from -1 to 2
- ridge_coef: float32 [64, 1024], P('sup'), may hold values from -1.5 to 1.5
Outputs:
- residual: float32 [64, 1024], P('tgt', 'sup')
- support_grad: float32 [64, 3, 1024], P('sup')
Inputs may be any that keep to these rules, and one draw needn't show every extreme that they name: `target_index`: any row of the pool; the first of each group's 32 targets lies in the pool rows of the devices half the tgt axis away.
All inputs are finite; a program needn't handle non-finite values.
Results may differ from a plain program's by a relative error of at most 0.0003.
Values may be sent and summed in bfloat16 or wider, within the bound.
A program may use at most 64 MiB of HBM per device.

v0:
```python
import math
import jax
import jax.numpy as jnp
from jax import lax
from jax.sharding import PartitionSpec as P

SIDE = 32
CHAN = 3
LAYERS = 4
WEIGHT_VAR = 2.0
BIAS_VAR = 0.1


def box_sum(values_map):
    column = jnp.arange(SIDE * SIDE) % SIDE
    zero_col = jnp.zeros(values_map.shape[:-1] + (1,), values_map.dtype)
    from_left = jnp.concatenate([zero_col, values_map[..., :-1]], -1)
    from_right = jnp.concatenate([values_map[..., 1:], zero_col], -1)
    row_sum = (
        values_map
        + jnp.where(column > 0, from_left, 0.0)
        + jnp.where(column < SIDE - 1, from_right, 0.0)
    )
    zero_row = jnp.zeros(values_map.shape[:-1] + (SIDE,), values_map.dtype)
    from_above = jnp.concatenate([zero_row, row_sum[..., :-SIDE]], -1)
    from_below = jnp.concatenate([row_sum[..., SIDE:], zero_row], -1)
    return (row_sum + from_above + from_below) / 9.0


def self_maps(pixels):
    current = jnp.sum(pixels * pixels, axis=1) / 3.0
    variances = []
    for depth in range(LAYERS):
        variance = WEIGHT_VAR * box_sum(current) + BIAS_VAR
        variances.append(variance)
        current = 2.0 / math.pi * jnp.arcsin(2.0 * variance / (1.0 + 2.0 * variance))
    return variances


def cross_layer(current, target_var, support_var):
    covariance = WEIGHT_VAR * box_sum(current) + BIAS_VAR
    denominator = jnp.sqrt(
        (1.0 + 2.0 * target_var)[:, None, :] * (1.0 + 2.0 * support_var)[None, :, :]
    )
    return 2.0 / math.pi * jnp.arcsin(2.0 * covariance / denominator)


def kernel_rows(targets, support, layer_step):
    target_vars = self_maps(targets)
    support_vars = self_maps(support)
    current = jnp.einsum("icp,jcp->ijp", targets, support, precision=lax.Precision.HIGHEST) / 3.0
    for depth in range(LAYERS):
        current = layer_step(current, target_vars[depth], support_vars[depth])
    return jnp.mean(current, axis=-1)


def local(image_pool, target_index, labels, support, ridge_coef):
    pool_rows = image_pool.shape[0]
    tgt_dev = labels.shape[0]
    flat_rank = lax.axis_index("tgt") * lax.axis_size("sup") + lax.axis_index("sup")
    owned_ids = flat_rank * pool_rows + jnp.arange(pool_rows, dtype=jnp.int32)
    selector = (target_index[:, None] == owned_ids[None, :]).astype(jnp.bfloat16)
    picked = jnp.dot(selector, image_pool, preferred_element_type=jnp.float32)
    every_target = lax.psum(picked, ("tgt", "sup"))
    group_pixels = lax.dynamic_slice_in_dim(
        every_target, lax.axis_index("tgt") * tgt_dev, tgt_dev, 0
    )
    targets = group_pixels.reshape(tgt_dev, CHAN, -1)
    layer_step = jax.checkpoint(cross_layer)
    kernel_block, pullback = jax.vjp(
        lambda points: kernel_rows(targets, points, layer_step), support
    )
    partial_value = jnp.dot(
        kernel_block,
        ridge_coef,
        precision=lax.Precision.HIGHEST,
        preferred_element_type=jnp.float32,
    )
    n_classes = ridge_coef.shape[1]
    per_owner = n_classes // lax.axis_size("sup")
    mine_pred = lax.psum_scatter(partial_value, "sup", scatter_dimension=1, tiled=True)
    class_start = lax.axis_index("sup") * per_owner
    target_hot = (
        labels[:, None] == class_start + jnp.arange(per_owner, dtype=jnp.int32)[None, :]
    ).astype(jnp.float32)
    residual = mine_pred - target_hot
    full_residual = lax.all_gather(residual, "sup", axis=1, tiled=True)
    loss_scale = float(SIDE * SIDE) / tgt_dev
    kernel_grad = loss_scale * jnp.dot(
        full_residual,
        ridge_coef.T,
        precision=lax.Precision.HIGHEST,
        preferred_element_type=jnp.float32,
    )
    local_grad = pullback(kernel_grad)[0]
    support_grad = lax.psum(local_grad, "tgt")
    return (residual, support_grad)


def solution(mesh):
    in_specs = (P(("tgt", "sup"), None), P(), P("tgt"), P("sup", None, None), P("sup", None))
    out_specs = (P("tgt", "sup"), P("sup", None, None))
    return jax.shard_map(local, mesh=mesh, in_specs=in_specs, out_specs=out_specs, check_vma=False)
```

profile of v0, /device:TPU:0, one launch (start us, length us, event | category | flops | bytes accessed | tf_op | source)
XLA Modules:
  0.0 323.5 jit_solution(5069627839205184832)
XLA Ops:
  7.3 0.9 copy-done
  8.2 1.8 fusion
  10.1 2.5 copy.79
  14.2 131.6 %all-reduce.98.cloned.1.call-done = f32[64,3072]{1,0:T(8,128)} async-done(((f32[64,3072]{1,0:T(8,128)}), f32[64,3072]{1,0:T(8,128)}) %all-reduce.98.cloned.1.call-update) | async-done | bytes 786448 | tf_op jit(solution)/shard_map/psum | solution.py:64
  145.8 1.0 constant_dynamic-slice_fusion
  146.9 0.3 reshape.46
  147.2 0.9 copy.78
  148.1 0.3 multiply_reduce_fusion.5
  148.4 9.9 %fusion.55 = f32[1024,32,4]{1,2,0:T(4,128)} fusion(f32[32,3,1024]{0,1,2:T(4,128)S(1)} %copy.78, f32[4,3,1024]{1,0,2:T(4,128)} %copy.79), kind=kOutput, calls=%fused_computation.181 | convolution fusion | flops 4718592 | bytes 966656 | tf_op jit(solution)/shard_map/jvp(icp,jcp->ijp)/dot_general | solution.py:51
  158.3 2.0 copy.80
  160.4 0.2 fusion.34
  160.6 0.2 select_add_fusion.7
  160.8 0.2 fusion.33
  161.3 0.4 add_multiply_fusion.9
  161.8 0.3 select_add_fusion.10
  162.1 1.2 add_multiply_fusion.6
  163.4 0.2 fusion.32
  163.6 0.2 select_add_fusion.6
  163.8 0.2 fusion.31
  164.1 0.4 add_multiply_fusion.8
  164.6 0.3 select_add_fusion.9
  164.9 1.2 add_multiply_fusion.5
  166.1 0.2 fusion.30
  166.3 0.2 select_add_fusion.5
  166.8 0.4 add_multiply_fusion.7
  167.3 0.3 select_add_fusion.8
  167.7 1.2 add_multiply_fusion.4
  168.9 0.2 fusion.28
  169.1 0.2 select_add_fusion.4
  169.8 1.3 multiply_reduce_fusion.4
  171.1 1.8 convolution_bitcast_fusion
  173.0 76.7 %reduce-scatter.4.cloned.1.call-done = f32[64,32]{1,0:T(8,128)} async-done(((f32[1024,32]{1,0:T(8,128)}), f32[64,32]{1,0:T(8,128)}) %reduce-scatter.4.cloned.1.call-update) | async-done | bytes 8208
  249.7 0.8 copy.95
  250.5 0.7 convert_subtract_fusion
  251.3 37.5 %all-gather = f32[16,64,32]{1,2,0:T(8,128)S(1)} all-gather(f32[1,64,32]{1,2,0:T(8,128)S(1)} %fusion.65), channel_id=1, replica_groups=mesh['tgt'=2,'sup'=16] {'sup'}, dimensions={0}, use_global_device_ids=true | all-gather | bytes 139264 | tf_op jit(solution)/shard_map/all_gather | solution.py:87
  289.6 0.2 select_add_fusion.3
  290.0 0.7 multiply_reduce_fusion
  290.7 0.2 fusion.24
  290.9 0.2 pad_add_fusion.6
  291.1 0.2 slice_select_fusion.7
  291.3 0.2 pad_add_fusion.5
  291.6 0.2 fusion.23
  291.8 0.2 select_add_fusion.2
  292.2 0.7 multiply_reduce_fusion.1
  292.9 0.2 fusion.21
  293.1 0.2 pad_add_fusion.4
  293.3 0.2 slice_select_fusion.5
  293.5 0.2 pad_add_fusion.3
  294.0 0.2 select_add_fusion.1
  294.4 0.7 multiply_reduce_fusion.2
  295.0 0.2 fusion.18
  295.2 0.2 pad_add_fusion.2
  295.5 0.2 slice_select_fusion.3
  295.7 0.2 pad_add_fusion.1
  296.1 0.2 select_add_fusion
  296.5 0.7 multiply_reduce_fusion.3
  297.2 0.2 fusion.15
  297.4 0.2 pad_add_fusion
  297.6 0.2 slice_select_fusion.1
  297.9 0.2 multiply_bitcast_fusion
  298.1 2.0 copy.83
  300.1 9.4 %fusion.56 = f32[1024,4,3]{1,2,0:T(4,128)} fusion(f32[1024,4,32]{2,1,0:T(4,128)} %copy.83, f32[32,3,1024]{0,1,2:T(4,128)S(1)} %copy-done.2), kind=kOutput, calls=%fused_computation.182 | convolution fusion | flops 4718592 | bytes 966656 | tf_op jit(solution)/shard_map/transpose(jvp(icp,jcp->ijp))/dot_general | solution.py:51
  309.4 1.8 copy.85
  312.6 4.1 %psum.15 = f32[4,3,1024]{2,0,1:T(4,128)} all-reduce(f32[4,3,1024]{2,0,1:T(4,128)S(1)} %add_add_fusion), channel_id=1, replica_groups=mesh['tgt'=2,'sup'=16] {'tgt'}, use_global_device_ids=true, to_apply=%region_9.10 | all-reduce | flops 12288 | bytes 98304 | tf_op jit(solution)/shard_map/psum | solution.py:96
  (92 shorter events, 6.8 us)
Async XLA Ops:
  7.2 1.0 copy-start
  7.2 5.4 %copy-start.3 = (f32[4,3,1024]{2,0,1:T(4,128)S(1)}, f32[4,3,1024]{2,0,1:T(4,128)}, u32[]{:S(2)}) copy-start(f32[4,3,1024]{2,0,1:T(4,128)} %param.8) | copy-start | bytes 147460
  7.2 138.6 %all-reduce.98.cloned.1.call-start = ((), (), s32[]{:S(2)}) async-start(), calls=%async_computation.1 | async-start | bytes 1572864 | tf_op jit(solution)/shard_map/psum | solution.py:64
  10.0 239.7 %reduce-scatter.4.cloned.1.call-start = ((), (), s32[]{:S(2)}) async-start(), calls=%async_computation.2 | async-start | bytes 557056
  148.0 10.2 %copy-start.1 = (f32[32,3,1024]{0,1,2:T(4,128)}, f32[32,3,1024]{0,1,2:T(4,128)S(1)}, u32[]{:S(2)}) copy-start(f32[32,3,1024]{0,1,2:T(4,128)S(1)} %copy.78) | copy-start | bytes 1179652
  169.3 1.8 copy-start.4
  169.5 81.0 %copy-start.5 = (s32[32]{0:T(128)S(1)}, s32[32]{0:T(128)}, u32[]{:S(2)}) copy-start(s32[32]{0:T(128)} %param.7) | copy-start | bytes 388
  297.9 2.2 copy-start.2
Sparse Core Ops, SparseCore 0:
  13.2 132.6 all-reduce.97
  173.1 76.5 reduce-scatter.3
where the time goes:
time: 324 us
  waiting for transfers between devices  208 us (64%)
  blocking collectives  41.6 us (13%)
  matrix products  23 us (7%)
  local copies, waits for them, and re-layouts  18.4 us (6%)
  other arithmetic  17.5 us (5%)
  between operations  14.6 us (5%)
    psum x1, waiting for transfers between devices, local(): every_target = lax.psum(picked, ('tgt', 'sup'))  132 us
    unnamed x3, waiting for transfers between devices  76.7 us
    all_gather x1, blocking collectives, local(): full_residual = lax.all_gather(residual, 'sup', axis=1, tiled=True)  37.5 us
    dot_general x2, matrix products, kernel_rows(): jnp.einsum('icp,jcp->ijp', targets, support, precision=lax.Precision.HIGH...  19.2 us
  transfers between devices with their start and end apart: 2, of which 2 were waited for; matrix products, arithmetic and copies ran while one was open for 1% of the time, Pallas kernels for 0%

commit v1 on v0

--- a/solution.py
+++ b/solution.py
@@ -3,6 +3,7 @@
 import jax.numpy as jnp
 from jax import lax
 from jax.sharding import PartitionSpec as P
+from jax.lax import all_gather
 
 SIDE = 32
 CHAN = 3
@@ -61,7 +62,8 @@
     owned_ids = flat_rank * pool_rows + jnp.arange(pool_rows, dtype=jnp.int32)
     selector = (target_index[:, None] == owned_ids[None, :]).astype(jnp.bfloat16)
     picked = jnp.dot(selector, image_pool, preferred_element_type=jnp.float32)
-    every_target = lax.psum(picked, ("tgt", "sup"))
+    move_loads = lambda mine_x, axis_tag: all_gather(mine_x, axis_tag).sum(axis=0)
+    every_target = move_loads(picked, ("tgt", "sup"))
     group_pixels = lax.dynamic_slice_in_dim(
         every_target, lax.axis_index("tgt") * tgt_dev, tgt_dev, 0
     )

time: 324 us -> 360 us (1.11)
  waiting for transfers between devices: 208 us -> 227 us
  other arithmetic: 17.5 us -> 32.3 us
  local copies, waits for them, and re-layouts: 18.4 us -> 22.3 us
    all_gather x0 -> x1, waiting for transfers between devices: none -> 151 us  [local(): all_gather(mine_x, axis_tag).sum(axis=0)]
    psum x1 -> x0, waiting for transfers between devices: 132 us -> none  [local(): every_target = lax.psum(picked, ('tgt', 'sup'))]
    reduce_sum x0 -> x1, other arithmetic: none -> 9.2 us  [local(): all_gather(mine_x, axis_tag).sum(axis=0)]
    unnamed x15 -> x61, local copies, waits for them, and re-layouts: 4.36 us -> 7.87 us
  transfers between devices with their start and end apart: 2 -> 2, of which waited for: 2 -> 2; matrix products, arithmetic and copies ran while one was open for 1% -> 2% of each run, Pallas kernels for 0% -> 0%
where the time goes in v1:
time: 360 us
  waiting for transfers between devices  227 us (63%)
  blocking collectives  41.8 us (12%)
  other arithmetic  32.3 us (9%)
  local copies, waits for them, and re-layouts  22.3 us (6%)
  matrix products  21.5 us (6%)
  between operations  14.7 us (4%)
    all_gather x1, waiting for transfers between devices, local(): all_gather(mine_x, axis_tag).sum(axis=0)  151 us
    unnamed x3, waiting for transfers between devices  75.9 us
    all_gather x1, blocking collectives, local(): full_residual = lax.all_gather(residual, 'sup', axis=1, tiled=True)  37.7 us
    dot_general x2, matrix products, kernel_rows(): jnp.einsum('icp,jcp->ijp', targets, support, precision=lax.Precision.HIGH...  17.7 us
    reduce_sum x1, other arithmetic, local(): all_gather(mine_x, axis_tag).sum(axis=0)  9.2 us
    unnamed x61, local copies, waits for them, and re-layouts  7.87 us
  transfers between devices with their start and end apart: 2, of which 2 were waited for; matrix products, arithmetic and copies ran while one was open for 2% of the time, Pallas kernels for 0%

profile of v1, /device:TPU:0, one launch (start us, length us, event | category | flops | bytes accessed | tf_op | source)
XLA Modules:
  0.0 359.5 jit_solution(7315359637862583473)
XLA Ops:
  7.3 0.9 copy-done
  8.2 1.8 fusion
  10.1 2.5 copy.79
  13.9 0.6 multiply_add_fusion.21
  14.5 0.6 multiply_add_fusion.23
  15.1 0.6 multiply_add_fusion.22
  15.9 0.7 multiply_add_fusion.16
  16.6 151.0 %all-gather.4.cloned.1.call-done = f32[2048,3072]{1,0:T(8,128)} async-done(((f32[64,3072]{1,0:T(8,128)}), f32[2048,3072]{1,0:T(8,128)}) %all-gather.4.cloned.1.call-update) | async-done | bytes 25165840 | tf_op jit(solution)/shard_map/all_gather | solution.py:65
  167.7 9.2 %reduce_sum.70 = f32[64,3072]{1,0:T(8,128)S(1)} reduce(f32[32,64,3072]{2,1,0:T(8,128)} %bitcast.27, f32[]{:T(128)} %constant.190.clone.1), dimensions={0}, to_apply=%region_0.0 | reduce | flops 6094848 | bytes 25952260 | tf_op jit(solution)/shard_map/reduce_sum | solution.py:65
  176.9 0.3 reshape.46
  177.2 0.3 multiply_reduce_fusion.5
  177.6 0.9 copy.78
  178.8 0.4 add_multiply_fusion.9
  179.3 0.9 select_add_fusion.10
  180.3 0.4 add_multiply_fusion.8
  180.8 0.9 select_add_fusion.9
  181.8 0.4 add_multiply_fusion.7
  182.3 0.9 select_add_fusion.8
  183.3 0.8 fusion.35
  184.0 8.2 %fusion.55 = f32[1024,32,4]{1,2,0:T(4,128)} fusion(f32[32,3,1024]{0,1,2:T(4,128)S(1)} %copy.78, f32[4,3,1024]{1,0,2:T(4,128)S(1)} %copy-done.4), kind=kOutput, calls=%fused_computation.181 | convolution fusion | flops 4718592 | bytes 966656 | tf_op jit(solution)/shard_map/jvp(icp,jcp->ijp)/dot_general | solution.py:52
  192.3 2.0 copy.80
  194.6 0.2 select_add_fusion.7
  195.0 0.5 copy-done.7
  195.5 1.2 add_multiply_fusion.6
  196.9 0.2 select_add_fusion.6
  197.3 0.5 copy-done.8
  197.8 1.2 add_multiply_fusion.5
  199.3 0.2 select_add_fusion.5
  199.7 0.5 copy-done.9
  200.2 1.2 add_multiply_fusion.4
  201.6 0.2 select_add_fusion.4
  202.0 0.4 copy-done.11
  202.5 0.8 multiply_add_fusion.4
  203.3 1.3 multiply_reduce_fusion.4
  204.7 1.8 convolution_bitcast_fusion
  206.6 75.8 %reduce-scatter.4.cloned.1.call-done = f32[64,32]{1,0:T(8,128)} async-done(((f32[1024,32]{1,0:T(8,128)}), f32[64,32]{1,0:T(8,128)}) %reduce-scatter.4.cloned.1.call-update) | async-done | bytes 8208
  282.4 0.8 copy.95
  283.3 0.7 convert_subtract_fusion
  284.0 37.7 %all-gather.1 = f32[16,64,32]{1,2,0:T(8,128)S(1)} all-gather(f32[1,64,32]{1,2,0:T(8,128)S(1)} %fusion.65), channel_id=1, replica_groups=mesh['tgt'=2,'sup'=16] {'sup'}, dimensions={0}, use_global_device_ids=true | all-gather | bytes 139264 | tf_op jit(solution)/shard_map/all_gather | solution.py:89
  322.5 0.2 select_add_fusion.3
  322.9 0.5 copy-done.10
  323.4 0.7 multiply_reduce_fusion
  324.5 0.2 pad_add_fusion.6
  324.8 0.2 slice_select_fusion.7
  325.4 0.2 select_add_fusion.2
  325.9 0.5 copy-done.6
  326.4 0.7 multiply_reduce_fusion.1
  327.6 0.2 pad_add_fusion.4
  327.8 0.2 slice_select_fusion.5
  328.4 0.2 select_add_fusion.1
  328.9 0.3 copy-done.18
  329.2 0.7 multiply_reduce_fusion.2
  330.3 0.2 pad_add_fusion.2
  330.6 0.2 slice_select_fusion.3
  331.2 0.2 select_add_fusion
  331.6 0.3 copy-done.16
  331.9 0.7 multiply_reduce_fusion.3
  333.1 0.2 pad_add_fusion
  333.3 0.2 slice_select_fusion.1
  333.6 1.0 multiply_bitcast_fusion
  334.6 2.6 copy.83
  337.2 9.4 %fusion.56 = f32[1024,4,3]{1,2,0:T(4,128)} fusion(f32[1024,4,32]{2,1,0:T(4,128)} %copy.83, f32[32,3,1024]{0,1,2:T(4,128)S(1)} %copy-done.3), kind=kOutput, calls=%fused_computation.182 | convolution fusion | flops 4718592 | bytes 966656 | tf_op jit(solution)/shard_map/transpose(jvp(icp,jcp->ijp))/dot_general | solution.py:52
  346.7 1.8 copy.85
  348.6 4.1 %psum.7 = f32[4,3,1024]{2,0,1:T(4,128)} all-reduce(f32[4,3,1024]{2,0,1:T(4,128)S(1)} %add_add_fusion), channel_id=1, replica_groups=mesh['tgt'=2,'sup'=16] {'tgt'}, use_global_device_ids=true, to_apply=%region_9.10 | all-reduce | flops 12288 | bytes 98304 | tf_op jit(solution)/shard_map/psum | solution.py:98
  (139 shorter events, 9.5 us)
Async XLA Ops:
  7.2 1.0 copy-start
  7.2 5.4 %copy-start.13 = (f32[4,3,1024]{2,0,1:T(4,128)S(1)}, f32[4,3,1024]{2,0,1:T(4,128)}, u32[]{:S(2)}) copy-start(f32[4,3,1024]{2,0,1:T(4,128)} %param.8) | copy-start | bytes 147460
  7.2 160.5 %all-gather.4.cloned.1.call-start = ((), (), s32[]{:S(2)}) async-start(), calls=%async_computation.1 | async-start | bytes 25952256 | tf_op jit(solution)/shard_map/all_gather | solution.py:65
  10.0 272.4 %reduce-scatter.4.cloned.1.call-start = ((), (), s32[]{:S(2)}) async-start(), calls=%async_computation.2 | async-start | bytes 557056
  13.0 154.7 %copy-start.15 = (f32[4,1024]{1,0:T(4,128)}, f32[4,1024]{1,0:T(4,128)S(1)}, u32[]{:S(2)}) copy-start(f32[4,1024]{1,0:T(4,128)S(1)} %get-tuple-element.33) | copy-start | bytes 49156
  13.4 154.2 %copy-start.17 = (f32[4,1024]{1,0:T(4,128)}, f32[4,1024]{1,0:T(4,128)S(1)}, u32[]{:S(2)}) copy-start(f32[4,1024]{1,0:T(4,128)S(1)} %get-tuple-element.29) | copy-start | bytes 49156
  13.9 153.8 %copy-start.19 = (f32[4,1024]{1,0:T(4,128)}, f32[4,1024]{1,0:T(4,128)S(1)}, u32[]{:S(2)}) copy-start(f32[4,1024]{1,0:T(4,128)S(1)} %get-tuple-element.25) | copy-start | bytes 49156
  178.4 5.6 %copy-start.2 = (f32[32,3,1024]{0,1,2:T(4,128)}, f32[32,3,1024]{0,1,2:T(4,128)S(1)}, u32[]{:S(2)}) copy-start(f32[32,3,1024]{0,1,2:T(4,128)S(1)} %copy.78) | copy-start | bytes 1179652
  180.7 3.3 copy-start.4
  182.2 10.0 %copy-start.5 = (f32[32,1024]{1,0:T(8,128)}, f32[32,1024]{1,0:T(8,128)S(1)}, u32[]{:S(2)}) copy-start(f32[32,1024]{1,0:T(8,128)S(1)} %get-tuple-element.24) | copy-start | bytes 393220
  194.6 0.9 copy-start.7
  194.6 0.9 copy-start.24
  196.9 0.9 copy-start.8
  196.9 0.9 copy-start.23
  199.2 0.9 copy-start.9
  199.2 0.9 copy-start.22
  201.6 0.9 copy-start.11
  201.6 1.0 copy-start.12
  201.6 1.7 copy-start.21
  201.8 2.8 copy-start.25
  202.0 81.2 %copy-start.28 = (s32[32]{0:T(128)S(1)}, s32[32]{0:T(128)}, u32[]{:S(2)}) copy-start(s32[32]{0:T(128)} %param.7) | copy-start | bytes 388
  203.3 118.6 %copy-start.26 = (f32[4,1024]{1,0:T(4,128)S(1)}, f32[4,1024]{1,0:T(4,128)}, u32[]{:S(2)}) copy-start(f32[4,1024]{1,0:T(4,128)} %param.9) | copy-start | bytes 49156
  322.5 0.9 copy-start.10
  322.5 0.9 copy-start.27
  325.4 0.9 copy-start.6
  325.4 0.9 copy-start.20
  328.4 0.7 copy-start.18
  331.2 0.7 copy-start.16
  333.6 3.7 %copy-start.3 = (f32[32,3,1024]{0,1,2:T(4,128)S(1)}, f32[32,3,1024]{0,1,2:T(4,128)}, u32[]{:S(2)}) copy-start(f32[32,3,1024]{0,1,2:T(4,128)} %copy-done.2) | copy-start | bytes 1179652
  337.2 15.5 %copy-start.1 = (bf16[64,3072]{1,0:T(8,128)(2,1)S(1)}, bf16[64,3072]{1,0:T(8,128)(2,1)}, u32[]{:S(2)}) copy-start(bf16[64,3072]{1,0:T(8,128)(2,1)} %param.5) | copy-start | bytes 1179652
  346.7 1.9 copy-start.14
Sparse Core Ops, SparseCore 0:
  10.9 156.7 all-gather.3
  206.6 75.7 reduce-scatter.3
